TPU v7x, 32 devices: a whole 2x2x4 slice. The times are simulated.
32 devices in a mesh: seq: 8 (over y, x, core), tp: 4 (over z).
Axes of the slice: x: 2, y: 2, z: 4, core: 2. Of those that a mesh axis runs over, the one named last changes fastest.
Arguments:
- layer_input: bfloat16 [8192, 2048], P('seq', 'tp'), may hold values from -18 to 18
- gain_one: float32 [2048], P('tp'), may hold values from 0.25 to 1.75
- query_weight: bfloat16 [2048, 2048], P('seq', 'tp'), may hold values from -0.13258252 to 0.13258252
- key_weight: bfloat16 [2048, 2048], P('seq', 'tp'), may hold values from -0.13258252 to 0.13258252
- value_weight: bfloat16 [2048, 4096], P('seq', 'tp'), may hold values from -0.13258252 to 0.13258252
- gate_weight: bfloat16 [2048, 4096], P('seq', 'tp'), may hold values from -0.13258252 to 0.13258252
- out_weight: bfloat16 [4096, 2048], P('tp', 'seq'), may hold values from -0.13258252 to 0.13258252
- gain_two: float32 [2048], P('tp'), may hold values from 0.25 to 1.75
- up_weight: bfloat16 [2048, 4096], P(None, 'tp'), may hold values from -0.13258252 to 0.13258252
- down_weight: bfloat16 [4096, 2048], P('tp'), may hold values from -0.13258252 to 0.13258252
- cotangent: bfloat16 [8192, 2048], P('seq', 'tp'), may hold values from -6 to 6
Outputs:
- layer_output: bfloat16 [8192, 2048], P('seq', 'tp')
- input_grad: bfloat16 [8192, 2048], P('seq', 'tp')
- gain_one_grad: float32 [2048], P('tp')
- query_weight_grad: float32 [2048, 2048], P('seq', 'tp')
- key_weight_grad: float32 [2048, 2048], P('seq', 'tp')
- value_weight_grad: float32 [2048, 4096], P('seq', 'tp')
- gate_weight_grad: float32 [2048, 4096], P('seq', 'tp')
- out_weight_grad: float32 [4096, 2048], P('tp', 'seq')
- gain_two_grad: float32 [2048], P('tp')
- up_weight_grad: float32 [2048, 4096], P(None, 'tp')
- down_weight_grad: float32 [4096, 2048], P('tp')
All inputs are finite; a program needn't handle non-finite values.
Results may differ from a plain program's by a relative error of at most 0.022.
Values may be sent and summed in bfloat16 or wider, within the bound.
No kernel may reach another device: no remote copies, remote signals or barrier semaphores. Data moves between devices by JAX's collectives and lax.ppermute only.
A program may use at most 192 MiB of HBM per device.

v0:
```python
import math
import jax
import jax.numpy as jnp
from jax import lax
from jax.sharding import PartitionSpec as P

D = 2048
KEY_DIM = 256
VAL_DIM = 512
BLOCK = 512
MAXLEN = 8192
norm_eps = 1e-05
group_eps = 1.0
highest_precision_mode = lax.Precision.HIGHEST


def entering(array, axis, join, neutral, backward):
    count = lax.axis_size(axis)
    place = lax.axis_index(axis)
    ahead = count - 1 - place if backward else place
    gathered = jax.tree.map(
        lambda a, kind: lax.all_gather(a.astype(kind), axis), array, (jnp.bfloat16, jnp.bfloat16)
    )
    state = jax.tree.map(lambda a, e: jnp.zeros_like(a) + jnp.asarray(e, a.dtype), array, neutral)

    def one(lap, state):
        source = count - 1 - lap if backward else lap
        return join(
            state,
            jax.tree.map(
                lambda a, own: lax.dynamic_index_in_dim(a, source, 0, False).astype(own.dtype),
                gathered,
                array,
            ),
        )

    return lax.fori_loop(0, ahead, one, state)


def feature_gather(tensor):
    return lax.all_gather(tensor, "tp", axis=1, tiled=True)


def feature_sum(tensor):
    return lax.psum_scatter(
        tensor.astype(jnp.bfloat16), "tp", scatter_dimension=1, tiled=True
    ).astype(jnp.float32)


def row_totals(linear, squared):
    return lax.psum((linear, squared), "tp")


def norm_forward(tensor):
    linear, squared = row_totals(jnp.sum(tensor, axis=1), jnp.sum(tensor * tensor, axis=1))
    average = linear / D
    factor = lax.rsqrt(squared / D - average * average + norm_eps)
    return ((tensor - average[:, None]) * factor[:, None], factor)


def norm_backward(upstream, gain_part, normed, factor):
    shaped = upstream * gain_part
    linear, squared = row_totals(jnp.sum(shaped, axis=1), jnp.sum(shaped * normed, axis=1))
    result = factor[:, None] * (shaped - linear[:, None] / D - normed * squared[:, None] / D)
    return (result, jnp.sum(upstream * normed, axis=0))


def rotary_tables(positions, halfway):
    frequency = jnp.exp(-math.log(10000.0) * jnp.arange(halfway, dtype=jnp.float32) / halfway)
    angles = positions.astype(jnp.float32)[:, None] * frequency[None, :]
    return (jnp.cos(angles), jnp.sin(angles))


def rotate(tensor, cosine, sine_table):
    halfway = tensor.shape[-1] // 2
    former = tensor[..., :halfway]
    latter = tensor[..., halfway:]
    cos_part = cosine[:, None, :]
    sin_part = sine_table[:, None, :]
    return jnp.concatenate(
        [former * cos_part - latter * sin_part, former * sin_part + latter * cos_part], axis=-1
    )


def rotate_back(tensor, cosine, sine_table):
    halfway = tensor.shape[-1] // 2
    former = tensor[..., :halfway]
    latter = tensor[..., halfway:]
    cos_part = cosine[:, None, :]
    sin_part = sine_table[:, None, :]
    return jnp.concatenate(
        [former * cos_part + latter * sin_part, latter * cos_part - former * sin_part], axis=-1
    )


def decay_tables(log_gamma, block_len):
    offsets = jnp.arange(block_len, dtype=jnp.float32)
    lagged = offsets[:, None] - offsets[None, :]
    within = jnp.where(
        lagged[None] >= 0.0, jnp.exp(jnp.maximum(lagged, 0.0)[None] * log_gamma[:, None, None]), 0.0
    )
    outward_result = jnp.exp((offsets + 1.0)[None, :] * log_gamma[:, None])
    inward = jnp.exp((block_len - 1.0 - offsets)[None, :] * log_gamma[:, None])
    return (within, outward_result.T, inward.T)


def gate_mix(gate_raw, retained, head_count):
    grouped = retained.reshape(retained.shape[0], head_count, -1)
    centered = grouped - jnp.mean(grouped, axis=-1, keepdims=True)
    normed = centered * lax.rsqrt(jnp.mean(centered * centered, axis=-1, keepdims=True) + group_eps)
    return jax.nn.silu(gate_raw) * normed.reshape(gate_raw.shape)


def compose(earlier, later):
    return (earlier[0] * later[0], later[0][:, None, None] * earlier[1] + later[1])


def local(
    layer_input,
    gain_one,
    query_weight,
    key_weight,
    value_weight,
    gate_weight,
    out_weight,
    gain_two,
    up_weight,
    down_weight,
    cotangent,
):
    tok_rows = layer_input.shape[0]
    head_count = query_weight.shape[1] // KEY_DIM
    block_count = tok_rows // BLOCK
    seq_devices = lax.axis_size("seq")
    seq_length = min(MAXLEN, tok_rows * seq_devices)
    own_index = lax.axis_index("seq")
    first_pos = own_index * tok_rows % seq_length
    carries = jnp.where(first_pos == 0, 0.0, 1.0).astype(jnp.float32)
    head_ids = lax.axis_index("tp") * head_count + jnp.arange(head_count)
    log_gamma = jnp.log(1.0 - jnp.exp2(-5.0 - head_ids.astype(jnp.float32)))
    within, outward_result, inward = decay_tables(log_gamma, BLOCK)
    block_decay_factor = jnp.exp(BLOCK * log_gamma)[:, None, None]
    device_decay = jnp.exp(tok_rows * log_gamma)
    block_steps = jnp.arange(block_count, dtype=jnp.float32)
    lead_decay = jnp.exp(block_steps[:, None] * BLOCK * log_gamma[None, :])
    tail_decay = jnp.exp((block_count - 1.0 - block_steps)[:, None] * BLOCK * log_gamma[None, :])
    out_scale = outward_result[None, :, :, None]
    in_scale = inward[None, :, :, None]
    positions = first_pos + jnp.arange(tok_rows)
    cosine, sine_table = rotary_tables(positions, KEY_DIM // 2)
    key_scale = 1.0 / math.sqrt(KEY_DIM)
    state_zeros = jnp.zeros((head_count, KEY_DIM, VAL_DIM), jnp.float32)
    x_float = layer_input.astype(jnp.float32)
    normed_one, factor_one = norm_forward(x_float)
    shared_one = feature_gather((normed_one * gain_one).astype(jnp.bfloat16))
    full_weights = (
        lax.all_gather(query_weight, "seq", axis=0, tiled=True),
        lax.all_gather(key_weight, "seq", axis=0, tiled=True),
        lax.all_gather(value_weight, "seq", axis=0, tiled=True),
        lax.all_gather(gate_weight, "seq", axis=0, tiled=True),
        lax.all_gather(out_weight, "seq", axis=1, tiled=True),
    )
    query_full, key_full, value_full, gate_full, out_full = full_weights
    query_raw = jnp.dot(shared_one, query_full, preferred_element_type=jnp.float32).reshape(
        tok_rows, head_count, KEY_DIM
    )
    key_raw = jnp.dot(shared_one, key_full, preferred_element_type=jnp.float32).reshape(
        tok_rows, head_count, KEY_DIM
    )
    query_low = rotate(query_raw, cosine, sine_table).astype(jnp.bfloat16)
    key_low = (rotate(key_raw, cosine, sine_table) * key_scale).astype(jnp.bfloat16)
    value_low = jnp.dot(shared_one, value_full, preferred_element_type=jnp.float32).astype(
        jnp.bfloat16
    )
    gate_raw = jnp.dot(shared_one, gate_full, preferred_element_type=jnp.float32)
    query_blocks = query_low.reshape(block_count, BLOCK, head_count, KEY_DIM)
    key_blocks = key_low.reshape(block_count, BLOCK, head_count, KEY_DIM)
    value_blocks = value_low.reshape(block_count, BLOCK, head_count, VAL_DIM)
    query_wide = query_blocks.astype(jnp.float32)
    value_wide = value_blocks.astype(jnp.float32)
    key_value_outer = in_scale * key_blocks.astype(jnp.float32)
    local_terms = jnp.einsum(
        "cmhk,cmhv->chkv", key_value_outer, value_wide, precision=highest_precision_mode
    )

    def advance(running, term):
        return (block_decay_factor * running + term, running)

    local_end, local_starts = lax.scan(advance, state_zeros, local_terms)
    identity = (jnp.ones((head_count,), jnp.float32), state_zeros)
    reached = entering((carries * device_decay, local_end), "seq", compose, identity, False)
    state_in = carries * reached[1]
    block_states = lead_decay[:, :, None, None] * state_in[None] + local_starts
    scores = jnp.einsum(
        "cnhk,cmhk->chnm", query_blocks, key_blocks, preferred_element_type=jnp.float32
    )
    weights = (scores * within[None]).astype(jnp.bfloat16)
    inside = jnp.einsum(
        "chnm,cmhv->cnhv", weights, value_blocks, preferred_element_type=jnp.float32
    )
    carried_state_sum = out_scale * jnp.einsum(
        "cnhk,chkv->cnhv", query_wide, block_states, precision=highest_precision_mode
    )
    retained = (inside + carried_state_sum).reshape(tok_rows, head_count * VAL_DIM)
    mixed = gate_mix(gate_raw, retained, head_count).astype(jnp.bfloat16)
    hidden = x_float + feature_sum(jnp.dot(mixed, out_full, preferred_element_type=jnp.float32))
    normed_two, factor_two = norm_forward(hidden)
    shared_local = (normed_two * gain_two).astype(jnp.bfloat16)
    cot_float = cotangent.astype(jnp.float32)
    shared_two = feature_gather(shared_local)
    cot_whole = feature_gather(cotangent)
    up_use, down_use = (up_weight, down_weight)
    up_pre = jnp.dot(shared_two, up_use, preferred_element_type=jnp.float32)
    activated = jax.nn.gelu(up_pre).astype(jnp.bfloat16)
    ffn_part = jnp.dot(activated, down_use, preferred_element_type=jnp.float32)
    ffn_out = feature_sum(ffn_part)
    result = hidden + ffn_out
    layer_output = result.astype(jnp.bfloat16)
    grad_act = jnp.einsum("rd,fd->rf", cot_whole, down_use, preferred_element_type=jnp.float32)
    down_grad = jnp.einsum("rf,rd->fd", activated, cot_whole, preferred_element_type=jnp.float32)
    _, gelu_pull = jax.vjp(jax.nn.gelu, up_pre)
    grad_up = gelu_pull(grad_act)[0].astype(jnp.bfloat16)
    up_grad = jnp.einsum("rd,rf->df", shared_two, grad_up, preferred_element_type=jnp.float32)
    grad_two_part = jnp.einsum("rf,df->rd", grad_up, up_use, preferred_element_type=jnp.float32)
    grad_two = feature_sum(grad_two_part)
    norm_two_back, gain_two_grad = norm_backward(grad_two, gain_two, normed_two, factor_two)
    grad_hidden = cot_float + norm_two_back
    grad_branch = feature_gather(grad_hidden.astype(jnp.bfloat16))
    query_back, key_back, value_back, gate_back, out_back = full_weights
    grad_mixed = jnp.einsum("rd,vd->rv", grad_branch, out_back, preferred_element_type=jnp.float32)
    out_grad = jnp.einsum("rv,rd->vd", mixed, grad_branch, preferred_element_type=jnp.float32)

    def gate_local(gate_input, retained_input):
        return gate_mix(gate_input, retained_input, head_count)

    _, mix_pull = jax.vjp(gate_local, gate_raw, retained)
    grad_gate_f, grad_retained_f = mix_pull(grad_mixed)
    grad_gate = grad_gate_f.astype(jnp.bfloat16)
    grad_out_blocks = grad_retained_f.astype(jnp.bfloat16).reshape(
        block_count, BLOCK, head_count, VAL_DIM
    )
    grad_out_wide = grad_out_blocks.astype(jnp.float32)
    scores_again = jnp.einsum(
        "cnhk,cmhk->chnm", query_blocks, key_blocks, preferred_element_type=jnp.float32
    )
    weights_again = (scores_again * within[None]).astype(jnp.bfloat16)
    grad_weights = jnp.einsum(
        "cnhv,cmhv->chnm", grad_out_blocks, value_blocks, preferred_element_type=jnp.float32
    )
    grad_scores = (grad_weights * within[None]).astype(jnp.bfloat16)
    grad_value = jnp.einsum(
        "chnm,cnhv->cmhv", weights_again, grad_out_blocks, preferred_element_type=jnp.float32
    )
    grad_query = jnp.einsum(
        "chnm,cmhk->cnhk", grad_scores, key_blocks, preferred_element_type=jnp.float32
    )
    grad_query = grad_query + out_scale * jnp.einsum(
        "cnhv,chkv->cnhk", grad_out_wide, block_states, precision=highest_precision_mode
    )
    grad_key = jnp.einsum(
        "chnm,cnhk->cmhk", grad_scores, query_blocks, preferred_element_type=jnp.float32
    )
    state_terms = jnp.einsum(
        "cnhk,cnhv->chkv", query_wide, out_scale * grad_out_wide, precision=highest_precision_mode
    )

    def retreat(running, term):
        updated = term + block_decay_factor * running
        return (updated, updated)

    _, local_grads = lax.scan(retreat, state_zeros, state_terms, reverse=True)
    local_first = local_grads[0]
    reached_back = entering(
        (carries * device_decay, carries * local_first), "seq", compose, identity, True
    )
    grad_end = reached_back[1]
    following = jnp.concatenate([local_grads[1:], jnp.zeros_like(local_grads[:1])], axis=0)
    grad_terms = following + tail_decay[:, :, None, None] * grad_end[None]
    grad_key = grad_key + in_scale * jnp.einsum(
        "cmhv,chkv->cmhk", value_wide, grad_terms, precision=highest_precision_mode
    )
    grad_value = grad_value + jnp.einsum(
        "cmhk,chkv->cmhv", key_value_outer, grad_terms, precision=highest_precision_mode
    )
    grad_query_raw = (
        rotate_back(grad_query.reshape(tok_rows, head_count, KEY_DIM), cosine, sine_table)
        .reshape(tok_rows, head_count * KEY_DIM)
        .astype(jnp.bfloat16)
    )
    grad_key_raw = (
        (
            rotate_back(grad_key.reshape(tok_rows, head_count, KEY_DIM), cosine, sine_table)
            * key_scale
        )
        .reshape(tok_rows, head_count * KEY_DIM)
        .astype(jnp.bfloat16)
    )
    grad_value_raw = grad_value.reshape(tok_rows, head_count * VAL_DIM).astype(jnp.bfloat16)
    query_grad = jnp.einsum(
        "rd,rk->dk", shared_one, grad_query_raw, preferred_element_type=jnp.float32
    )
    key_grad = jnp.einsum("rd,rk->dk", shared_one, grad_key_raw, preferred_element_type=jnp.float32)
    value_grad = jnp.einsum(
        "rd,rv->dv", shared_one, grad_value_raw, preferred_element_type=jnp.float32
    )
    gate_grad = jnp.einsum("rd,rv->dv", shared_one, grad_gate, preferred_element_type=jnp.float32)
    grad_shared = jnp.einsum(
        "rk,dk->rd", grad_query_raw, query_back, preferred_element_type=jnp.float32
    )
    grad_shared = grad_shared + jnp.einsum(
        "rk,dk->rd", grad_key_raw, key_back, preferred_element_type=jnp.float32
    )
    grad_shared = grad_shared + jnp.einsum(
        "rv,dv->rd", grad_value_raw, value_back, preferred_element_type=jnp.float32
    )
    grad_shared = grad_shared + jnp.einsum(
        "rv,dv->rd", grad_gate, gate_back, preferred_element_type=jnp.float32
    )
    grad_one = feature_sum(grad_shared)
    norm_one_back, gain_one_grad = norm_backward(grad_one, gain_one, normed_one, factor_one)
    input_grad = (grad_hidden + norm_one_back).astype(jnp.bfloat16)
    mixer_sums = (
        lax.psum_scatter(
            query_grad.astype(jnp.bfloat16), "seq", scatter_dimension=0, tiled=True
        ).astype(jnp.float32),
        lax.psum_scatter(
            key_grad.astype(jnp.bfloat16), "seq", scatter_dimension=0, tiled=True
        ).astype(jnp.float32),
        lax.psum_scatter(
            value_grad.astype(jnp.bfloat16), "seq", scatter_dimension=0, tiled=True
        ).astype(jnp.float32),
        lax.psum_scatter(
            gate_grad.astype(jnp.bfloat16), "seq", scatter_dimension=0, tiled=True
        ).astype(jnp.float32),
        lax.psum_scatter(
            out_grad.astype(jnp.bfloat16), "seq", scatter_dimension=1, tiled=True
        ).astype(jnp.float32),
    )
    ffn_sums = (
        lax.psum(up_grad.astype(jnp.bfloat16), "seq").astype(jnp.float32),
        lax.psum(down_grad.astype(jnp.bfloat16), "seq").astype(jnp.float32),
        lax.psum(gain_one_grad.astype(jnp.bfloat16), "seq").astype(jnp.float32),
        lax.psum(gain_two_grad.astype(jnp.bfloat16), "seq").astype(jnp.float32),
    )
    return (
        layer_output,
        input_grad,
        ffn_sums[2],
        mixer_sums[0],
        mixer_sums[1],
        mixer_sums[2],
        mixer_sums[3],
        mixer_sums[4],
        ffn_sums[3],
        ffn_sums[0],
        ffn_sums[1],
    )


def solution(mesh):
    placed = (
        P("seq", "tp"),
        P("tp"),
        P("seq", "tp"),
        P("seq", "tp"),
        P("seq", "tp"),
        P("seq", "tp"),
        P("tp", "seq"),
        P("tp"),
        P(None, "tp"),
        P("tp", None),
        P("seq", "tp"),
    )
    return jax.shard_map(
        local,
        mesh=mesh,
        in_specs=placed,
        out_specs=(
            P("seq", "tp"),
            P("seq", "tp"),
            P("tp"),
            P("seq", "tp"),
            P("seq", "tp"),
            P("seq", "tp"),
            P("seq", "tp"),
            P("tp", "seq"),
            P("tp"),
            P(None, "tp"),
            P("tp", None),
        ),
        check_vma=False,
    )
```

profile of v0, /device:TPU:0, one launch (start us, length us, event | category | flops | bytes accessed | tf_op | source)
XLA Modules:
  0.0 1420.9 jit_solution(11341853395114596802)
XLA Ops:
  9.6 13.7 all-reduce.4
  29.5 11.0 all-gather.22.cloned.1.call-done
  40.4 82.9 %all-gather.14.cloned.1.call-done = bf16[1024,2048]{1,0:T(8,128)(2,1)} async-done(((bf16[1024,512]{1,0:T(8,128)(2,1)}), bf16[1024,2048]{1,0:T(8,128)(2,1)}) %all-gather.14.cloned.1.call-update) | async-done | bytes 4194320 | tf_op jit(solution)/shard_map/all_gather | solution.py:41
  123.3 5.2 fusion.84
  133.7 17.9 %all-gather.20.cloned.1.call-done = bf16[2048,512]{1,0:T(8,128)(2,1)} async-done(((bf16[256,512]{1,0:T(8,128)(2,1)}), bf16[2048,512]{1,0:T(8,128)(2,1)}) %all-gather.20.cloned.1.call-update) | async-done | bytes 2097168 | tf_op jit(solution)/shard_map/all_gather | solution.py:157
  151.5 5.2 fusion.83
  166.6 23.2 %all-gather.18.cloned.1.call-done = bf16[2048,1024]{1,0:T(8,128)(2,1)} async-done(((bf16[256,1024]{1,0:T(8,128)(2,1)}), bf16[2048,1024]{1,0:T(8,128)(2,1)}) %all-gather.18.cloned.1.call-update) | async-done | bytes 4194320 | tf_op jit(solution)/shard_map/all_gather | solution.py:159
  189.9 9.3 convolution_convert_fusion.10
  202.6 4.8 fusion.50
  209.0 4.6 while.58
  215.9 8.7 all-gather.1
  232.0 19.3 %all-gather.34.cloned.1.call-done = bf16[16,256,512]{2,1,0:T(8,128)(2,1)} async-done(((bf16[2,256,512]{2,1,0:T(8,128)(2,1)}), bf16[16,256,512]{2,1,0:T(8,128)(2,1)}) %all-gather.34.cloned.1.call-update) | async-done | bytes 4194320 | tf_op jit(solution)/shard_map/all_gather | solution.py:22
  253.3 7.1 fusion.82
  260.5 7.6 copy.152
  274.5 15.1 %all-gather.16.cloned.1.call-done = bf16[2048,1024]{1,0:T(8,128)(2,1)} async-done(((bf16[256,1024]{1,0:T(8,128)(2,1)}), bf16[2048,1024]{1,0:T(8,128)(2,1)}) %all-gather.16.cloned.1.call-update) | async-done | bytes 4194320 | tf_op jit(solution)/shard_map/all_gather | solution.py:160
  289.6 12.8 multiply_convert_fusion.2
  302.4 26.5 %all-gather.24.cloned.1.call-done = bf16[1024,2048]{1,0:T(8,128)(2,1)} async-done(((bf16[1024,256]{1,0:T(8,128)(2,1)}), bf16[1024,2048]{1,0:T(8,128)(2,1)}) %all-gather.24.cloned.1.call-update) | async-done | bytes 4194320 | tf_op jit(solution)/shard_map/all_gather | solution.py:161
  328.8 9.4 convolution_convert_fusion.7
  339.5 75.8 %reduce-scatter.10.cloned.1.call-done = bf16[1024,512]{1,0:T(8,128)(2,1)} async-done(((bf16[1024,2048]{1,0:T(8,128)(2,1)}), bf16[1024,512]{1,0:T(8,128)(2,1)}) %reduce-scatter.10.cloned.1.call-update) | async-done | bytes 1048592 | tf_op jit(solution)/shard_map/reduce_scatter | solution.py:45
  417.0 11.1 all-reduce.3
  430.9 67.2 %all-gather.28.cloned.1.call-done = bf16[1024,2048]{1,0:T(8,128)(2,1)} async-done(((bf16[1024,512]{1,0:T(8,128)(2,1)}), bf16[1024,2048]{1,0:T(8,128)(2,1)}) %all-gather.28.cloned.1.call-update) | async-done | bytes 4194320 | tf_op jit(solution)/shard_map/all_gather | solution.py:41
  498.1 10.1 fusion.85
  508.1 71.2 %all-gather.26.cloned.1.call-done = bf16[1024,2048]{1,0:T(8,128)(2,1)} async-done(((bf16[1024,512]{1,0:T(8,128)(2,1)}), bf16[1024,2048]{1,0:T(8,128)(2,1)}) %all-gather.26.cloned.1.call-update) | async-done | bytes 4194320 | tf_op jit(solution)/shard_map/all_gather | solution.py:41
  579.3 13.9 fusion.10
  594.5 6.3 convolution_convert_fusion.5
  600.9 75.4 %reduce-scatter.14.cloned.1.call-done = bf16[1024,512]{1,0:T(8,128)(2,1)} async-done(((bf16[1024,2048]{1,0:T(8,128)(2,1)}), bf16[1024,512]{1,0:T(8,128)(2,1)}) %reduce-scatter.14.cloned.1.call-update) | async-done | bytes 1048592 | tf_op jit(solution)/shard_map/reduce_scatter | solution.py:45
  680.1 11.1 all-reduce.2
  695.2 4.6 copy.163
  699.8 74.6 %all-gather.30.cloned.1.call-done = bf16[1024,2048]{1,0:T(8,128)(2,1)} async-done(((bf16[1024,512]{1,0:T(8,128)(2,1)}), bf16[1024,2048]{1,0:T(8,128)(2,1)}) %all-gather.30.cloned.1.call-update) | async-done | bytes 4194320 | tf_op jit(solution)/shard_map/all_gather | solution.py:41
  774.4 14.5 %fusion.72 = (f32[1024,1024]{0,1:T(8,128)}, bf16[1024,1024]{0,1:T(8,128)(2,1)}) fusion(f32[1024,1024]{0,1:T(8,128)} %get-tuple-element.456, f32[1024,2]{0,1:T(2,128)S(1)} %rsqrt.18, f32[1024,1024]{0,1:T(8,128)} %bitcast.171, f32[1024,2]{0,1:T(2,128)S(1)} %bitcast.198, bf16[1024,2048]{1,0:T(8,128)(2,1)} %all-gather.30.cloned.1.call-done, ...), kind=kOutput, calls=%fused_computation.147 | convolution fusion | flops 4310695936 | bytes 23085056 | tf_op jit(solution)/shard_map/rd,vd->rv/dot_general | solution.py:230
  789.0 5.6 copy.164
  794.6 4.4 multiply_reduce_fusion
  806.5 4.5 reshape.451
  810.9 6.1 copy.167
  817.1 5.9 fusion.18
  824.6 5.3 while.59
  832.9 9.5 convolution_convert_fusion.1
  842.4 6.8 convolution_convert_fusion
  849.3 9.4 convolution_convert_fusion.2
  858.8 9.5 convolution_convert_fusion.3
  869.6 4.3 fusion.52
  881.8 9.9 while.57
  901.1 6.4 convolution_convert_fusion.9
  911.7 6.0 convolution_convert_fusion.8
  922.4 7.5 fusion.54
  936.7 6.3 convolution_convert_fusion.4
  944.6 6.5 fusion.89
  951.2 5.8 fusion.86
  957.0 6.8 fusion.88
  963.8 11.7 add_convert_fusion
  975.7 10.8 convolution_convert_fusion.6
  986.6 11.3 all-reduce.9.cloned.1.call-done
  997.9 6.8 convert_element_type.309
  1004.7 4.7 convert_element_type.311
  1009.4 42.9 %reduce-scatter.26.cloned.1.call-done = bf16[1024,256]{1,0:T(8,128)(2,1)} async-done(((bf16[1024,2048]{1,0:T(8,128)(2,1)}), bf16[1024,256]{1,0:T(8,128)(2,1)}) %reduce-scatter.26.cloned.1.call-update) | async-done | bytes 524304 | tf_op jit(solution)/shard_map/reduce_scatter | solution.py:335
  1054.4 52.3 %reduce-scatter.24.cloned.1.call-done = bf16[256,1024]{1,0:T(8,128)(2,1)} async-done(((bf16[2048,1024]{1,0:T(8,128)(2,1)}), bf16[256,1024]{1,0:T(8,128)(2,1)}) %reduce-scatter.24.cloned.1.call-update) | async-done | bytes 524304 | tf_op jit(solution)/shard_map/reduce_scatter | solution.py:332
  1108.8 42.1 %reduce-scatter.18.cloned.1.call-done = bf16[256,512]{1,0:T(8,128)(2,1)} async-done(((bf16[2048,512]{1,0:T(8,128)(2,1)}), bf16[256,512]{1,0:T(8,128)(2,1)}) %reduce-scatter.18.cloned.1.call-update) | async-done | bytes 262160 | tf_op jit(solution)/shard_map/reduce_scatter | solution.py:323
  1152.8 42.4 %reduce-scatter.20.cloned.1.call-done = bf16[256,512]{1,0:T(8,128)(2,1)} async-done(((bf16[2048,512]{1,0:T(8,128)(2,1)}), bf16[256,512]{1,0:T(8,128)(2,1)}) %reduce-scatter.20.cloned.1.call-update) | async-done | bytes 262160 | tf_op jit(solution)/shard_map/reduce_scatter | solution.py:326
  1197.0 52.7 %reduce-scatter.22.cloned.1.call-done = bf16[256,1024]{1,0:T(8,128)(2,1)} async-done(((bf16[2048,1024]{1,0:T(8,128)(2,1)}), bf16[256,1024]{1,0:T(8,128)(2,1)}) %reduce-scatter.22.cloned.1.call-update) | async-done | bytes 524304 | tf_op jit(solution)/shard_map/reduce_scatter | solution.py:329
  1251.8 76.8 %reduce-scatter.16.cloned.1.call-done = bf16[1024,512]{1,0:T(8,128)(2,1)} async-done(((bf16[1024,2048]{1,0:T(8,128)(2,1)}), bf16[1024,512]{1,0:T(8,128)(2,1)}) %reduce-scatter.16.cloned.1.call-update) | async-done | bytes 1048592 | tf_op jit(solution)/shard_map/reduce_scatter | solution.py:45
  1331.3 13.4 all-reduce.5
  1345.8 12.3 all-reduce.1
  1358.1 50.7 %reduce-scatter.12.cloned.1.call-done = bf16[1024,512]{1,0:T(8,128)(2,1)} async-done(((bf16[1024,2048]{1,0:T(8,128)(2,1)}), bf16[1024,512]{1,0:T(8,128)(2,1)}) %reduce-scatter.12.cloned.1.call-update) | async-done | bytes 1048592 | tf_op jit(solution)/shard_map/reduce_scatter | solution.py:45
  1408.9 5.0 fusion.36
  (279 shorter events, 142.5 us)
Async XLA Ops:
  7.2 33.2 %all-gather.22.cloned.1.call-start = ((), (), s32[]{:S(2)}) async-start(), calls=%async_computation.13 | async-start | bytes 2359296 | tf_op jit(solution)/shard_map/all_gather | solution.py:158
  7.9 115.4 %all-gather.14.cloned.1.call-start = ((), (), s32[]{:S(2)}) async-start(), calls=%async_computation.9 | async-start | bytes 5242880 | tf_op jit(solution)/shard_map/all_gather | solution.py:41
  23.3 4.1 copy-start.49
  23.3 4.1 copy-start.51
  26.0 125.5 %all-gather.20.cloned.1.call-start = ((), (), s32[]{:S(2)}) async-start(), calls=%async_computation.12 | async-start | bytes 2359296 | tf_op jit(solution)/shard_map/all_gather | solution.py:157
  26.7 163.2 %all-gather.18.cloned.1.call-start = ((), (), s32[]{:S(2)}) async-start(), calls=%async_computation.11 | async-start | bytes 4718592 | tf_op jit(solution)/shard_map/all_gather | solution.py:159
  27.3 223.9 %all-gather.34.cloned.1.call-start = ((), (), s32[]{:S(2)}) async-start(), calls=%async_computation.28 | async-start | bytes 4718592 | tf_op jit(solution)/shard_map/all_gather | solution.py:22
  27.5 175.1 %copy-start.43 = (f32[512,2]{0,1:T(2,128)}, f32[512,2]{0,1:T(2,128)S(1)}, u32[]{:S(2)}) copy-start(f32[512,2]{0,1:T(2,128)S(1)} %get-tuple-element.451) | copy-start | bytes 12292
  29.4 132.4 %copy-start.29 = (f32[1024,128]{1,0:T(8,128)}, f32[1024,128]{1,0:T(8,128)S(1)}, u32[]{:S(2)}) copy-start(f32[1024,128]{1,0:T(8,128)S(1)} %get-tuple-element.443) | copy-start | bytes 1572868
  29.4 132.4 %copy-start.31 = (f32[1024,128]{1,0:T(8,128)}, f32[1024,128]{1,0:T(8,128)S(1)}, u32[]{:S(2)}) copy-start(f32[1024,128]{1,0:T(8,128)S(1)} %get-tuple-element.444) | copy-start | bytes 1572868
  214.5 75.1 %all-gather.16.cloned.1.call-start = ((), (), s32[]{:S(2)}) async-start(), calls=%async_computation.10 | async-start | bytes 4718592 | tf_op jit(solution)/shard_map/all_gather | solution.py:160
  215.1 113.8 %all-gather.24.cloned.1.call-start = ((), (), s32[]{:S(2)}) async-start(), calls=%async_computation.14 | async-start | bytes 4718592 | tf_op jit(solution)/shard_map/all_gather | solution.py:161
  215.8 199.4 %reduce-scatter.10.cloned.1.call-start = ((), (), s32[]{:S(2)}) async-start(), calls=%async_computation.15 | async-start | bytes 5242880 | tf_op jit(solution)/shard_map/reduce_scatter | solution.py:45
  251.5 9.0 copy-start.10
  338.3 77.0 %copy-start.1 = (bf16[1024,512]{1,0:T(8,128)(2,1)S(1)}, bf16[1024,512]{1,0:T(8,128)(2,1)}, u32[]{:S(2)}) copy-start(bf16[1024,512]{1,0:T(8,128)(2,1)} %param.19) | copy-start | bytes 3145732
  338.3 89.8 %copy-start.55 = (f32[512]{0:T(512)S(1)}, f32[512]{0:T(512)}, u32[]{:S(2)}) copy-start(f32[512]{0:T(512)} %param.26) | copy-start | bytes 6148
  338.3 159.8 %all-gather.28.cloned.1.call-start = ((), (), s32[]{:S(2)}) async-start(), calls=%async_computation.18 | async-start | bytes 5242880 | tf_op jit(solution)/shard_map/all_gather | solution.py:41
  339.0 240.3 %all-gather.26.cloned.1.call-start = ((), (), s32[]{:S(2)}) async-start(), calls=%async_computation.16 | async-start | bytes 5242880 | tf_op jit(solution)/shard_map/all_gather | solution.py:41
  428.1 263.1 %copy-start.45 = (f32[1024]{0:T(1024)}, f32[1024]{0:T(1024)S(1)}, u32[]{:S(2)}) copy-start(f32[1024]{0:T(1024)S(1)} %get-tuple-element.445) | copy-start | bytes 12292
  428.1 263.1 %copy-start.47 = (f32[1024]{0:T(1024)}, f32[1024]{0:T(1024)S(1)}, u32[]{:S(2)}) copy-start(f32[1024]{0:T(1024)S(1)} %get-tuple-element.446) | copy-start | bytes 12292
  430.8 245.5 %reduce-scatter.14.cloned.1.call-start = ((), (), s32[]{:S(2)}) async-start(), calls=%async_computation.19 | async-start | bytes 5242880 | tf_op jit(solution)/shard_map/reduce_scatter | solution.py:45
  579.3 15.2 %copy-start.61 = (bf16[2048,1024]{1,0:T(8,128)(2,1)S(1)}, bf16[2048,1024]{1,0:T(8,128)(2,1)}, u32[]{:S(2)}) copy-start(bf16[2048,1024]{1,0:T(8,128)(2,1)} %param.27) | copy-start | bytes 12582916
  600.9 173.6 %all-gather.30.cloned.1.call-start = ((), (), s32[]{:S(2)}) async-start(), calls=%async_computation.20 | async-start | bytes 5242880 | tf_op jit(solution)/shard_map/all_gather | solution.py:41
  691.2 4.0 copy-start.58
  695.2 186.5 %all-gather.32.cloned.1.call-start = ((), (), s32[]{:S(2)}) async-start(), calls=%async_computation.21 | async-start | bytes 4718592 | tf_op jit(solution)/shard_map/all_gather | solution.py:22
  794.6 4.6 copy-start.6
  794.6 5.9 copy-start.7
  800.5 3.5 copy-start.5
  832.8 165.0 %all-reduce.9.cloned.1.call-start = ((), (), s32[]{:S(2)}) async-start(), calls=%async_computation.29 | async-start | bytes 16777216 | tf_op jit(solution)/shard_map/psum | solution.py:340
  832.9 9.6 copy-start.63
  832.9 9.6 copy-start.65
  849.3 203.0 %reduce-scatter.26.cloned.1.call-start = ((), (), s32[]{:S(2)}) async-start(), calls=%async_computation.27 | async-start | bytes 4718592 | tf_op jit(solution)/shard_map/reduce_scatter | solution.py:335
  858.8 247.9 %reduce-scatter.24.cloned.1.call-start = ((), (), s32[]{:S(2)}) async-start(), calls=%async_computation.26 | async-start | bytes 4718592 | tf_op jit(solution)/shard_map/reduce_scatter | solution.py:332
  868.4 282.5 %reduce-scatter.18.cloned.1.call-start = ((), (), s32[]{:S(2)}) async-start(), calls=%async_computation.23 | async-start | bytes 2359296 | tf_op jit(solution)/shard_map/reduce_scatter | solution.py:323
  869.6 4.3 copy-start.4
  869.6 4.3 copy-start.8
  891.7 3.6 copy-start.19
  891.7 3.6 copy-start.25
  891.8 3.6 copy-start.27
  891.8 3.6 copy-start.44
  901.1 6.4 copy-start.41
  907.5 287.6 %reduce-scatter.20.cloned.1.call-start = ((), (), s32[]{:S(2)}) async-start(), calls=%async_computation.24 | async-start | bytes 2359296 | tf_op jit(solution)/shard_map/reduce_scatter | solution.py:326
  917.7 332.0 %reduce-scatter.22.cloned.1.call-start = ((), (), s32[]{:S(2)}) async-start(), calls=%async_computation.25 | async-start | bytes 4718592 | tf_op jit(solution)/shard_map/reduce_scatter | solution.py:329
  936.2 6.8 copy-start.39
  943.0 385.7 %reduce-scatter.16.cloned.1.call-start = ((), (), s32[]{:S(2)}) async-start(), calls=%async_computation.22 | async-start | bytes 5242880 | tf_op jit(solution)/shard_map/reduce_scatter | solution.py:45
  944.6 6.5 copy-start.42
  944.6 6.6 copy-start.64
  951.2 5.8 copy-start.40
  951.2 5.8 copy-start.62
  957.0 6.8 copy-start.35
  975.5 433.3 %reduce-scatter.12.cloned.1.call-start = ((), (), s32[]{:S(2)}) async-start(), calls=%async_computation.17 | async-start | bytes 5242880 | tf_op jit(solution)/shard_map/reduce_scatter | solution.py:45
  997.9 6.8 copy-start.33
  1054.4 274.3 %copy-start.2 = (bf16[1024,512]{1,0:T(8,128)(2,1)S(1)}, bf16[1024,512]{1,0:T(8,128)(2,1)}, u32[]{:S(2)}) copy-start(bf16[1024,512]{1,0:T(8,128)(2,1)} %param.19) | copy-start | bytes 3145732
  1054.4 274.3 %copy-start.50 = (f32[1024]{0:T(1024)S(1)}, f32[1024]{0:T(1024)}, u32[]{:S(2)}) copy-start(f32[1024]{0:T(1024)} %copy-done.49) | copy-start | bytes 12292
  1054.4 274.3 %copy-start.52 = (f32[1024]{0:T(1024)S(1)}, f32[1024]{0:T(1024)}, u32[]{:S(2)}) copy-start(f32[1024]{0:T(1024)} %copy-done.51) | copy-start | bytes 12292
  1054.4 274.3 %copy-start.57 = (f32[512]{0:T(512)S(1)}, f32[512]{0:T(512)}, u32[]{:S(2)}) copy-start(f32[512]{0:T(512)} %param.20) | copy-start | bytes 6148
  1152.7 178.6 %copy-start.60 = (bf16[512]{0:T(512)(128)(2,1)S(1)}, bf16[512]{0:T(512)(128)(2,1)}, u32[]{:S(2)}) copy-start(bf16[512]{0:T(512)(128)(2,1)} %get-tuple-element.357) | copy-start | bytes 3076
  1152.7 256.1 %copy-start.15 = (bf16[1024,512]{1,0:T(8,128)(2,1)S(1)}, bf16[1024,512]{1,0:T(8,128)(2,1)}, u32[]{:S(2)}) copy-start(bf16[1024,512]{1,0:T(8,128)(2,1)} %reduce-scatter.10.cloned.1.call-done) | copy-start | bytes 3145732
  1152.7 256.1 %copy-start.22 = (bf16[1024,512]{1,0:T(8,128)(2,1)S(1)}, bf16[1024,512]{1,0:T(8,128)(2,1)}, u32[]{:S(2)}) copy-start(bf16[1024,512]{1,0:T(8,128)(2,1)} %reduce-scatter.14.cloned.1.call-done) | copy-start | bytes 3145732
  1152.7 256.1 %copy-start.46 = (f32[1024]{0:T(1024)S(1)}, f32[1024]{0:T(1024)}, u32[]{:S(2)}) copy-start(f32[1024]{0:T(1024)} %copy-done.45) | copy-start | bytes 12292
  1152.7 256.1 %copy-start.48 = (f32[1024]{0:T(1024)S(1)}, f32[1024]{0:T(1024)}, u32[]{:S(2)}) copy-start(f32[1024]{0:T(1024)} %copy-done.47) | copy-start | bytes 12292
  1152.7 256.1 %copy-start.54 = (f32[1024]{0:T(1024)S(1)}, f32[1024]{0:T(1024)}, u32[]{:S(2)}) copy-start(f32[1024]{0:T(1024)} %copy-done.53) | copy-start | bytes 12292
  1152.8 256.1 %copy-start.56 = (f32[512]{0:T(512)S(1)}, f32[512]{0:T(512)}, u32[]{:S(2)}) copy-start(f32[512]{0:T(512)} %param.26) | copy-start | bytes 6148
  1152.8 256.1 %copy-start.59 = (f32[1024]{0:T(1024)S(1)}, f32[1024]{0:T(1024)}, u32[]{:S(2)}) copy-start(f32[1024]{0:T(1024)} %copy-done.58) | copy-start | bytes 12292
  (25 other events, 46.1 us)
Sparse Core Ops, SparseCore 0:
  9.9 30.5 all-gather.21
  42.6 80.7 all-gather.13
  125.2 26.2 all-gather.19
  153.3 36.5 all-gather.17
  214.6 36.5 all-gather.33
  253.0 36.5 all-gather.15
  291.5 37.3 all-gather.23
  338.4 76.7 reduce-scatter.9
  416.8 81.2 all-gather.27
  500.1 79.2 all-gather.25
  601.0 75.2 reduce-scatter.13
  695.3 79.0 all-gather.29
  832.9 35.0 all-gather.31
  871.6 126.2 all-reduce.8
  1001.1 51.1 reduce-scatter.25
  1055.5 51.1 reduce-scatter.23
  1109.8 41.0 reduce-scatter.17
  1154.1 41.0 reduce-scatter.19
  1198.5 51.1 reduce-scatter.21
  1251.9 76.7 reduce-scatter.15
  1331.0 77.7 reduce-scatter.11
where the time goes:
time: 1430 us; the launch traced here: 1420 us
  waiting for transfers between devices  935 us (65%)
  matrix products  227 us (16%)
  other arithmetic  90.3 us (6%)
  local copies, waits for them, and re-layouts  79.9 us (6%)
  blocking collectives  70.4 us (5%)
  between operations  15.5 us (1%)
    all_gather x4, waiting for transfers between devices, feature_gather(): return lax.all_gather(tensor, 'tp', axis=1, tiled=True)  296 us
    reduce_scatter x4, waiting for transfers between devices, feature_sum(): lax.psum_scatter(tensor.astype(jnp.bfloat16), 'tp', scatter_dimension=1,...  279 us
    reduce_scatter x1, waiting for transfers between devices, local(): lax.psum_scatter(value_grad.astype(jnp.bfloat16), 'seq', scatter_dimensio...  52.7 us
    reduce_scatter x1, waiting for transfers between devices, local(): lax.psum_scatter(gate_grad.astype(jnp.bfloat16), 'seq', scatter_dimension...  52.3 us
    psum x4, blocking collectives, row_totals(): return lax.psum((linear, squared), 'tp')  48.3 us
    reduce_scatter x1, waiting for transfers between devices, local(): lax.psum_scatter(out_grad.astype(jnp.bfloat16), 'seq', scatter_dimension=...  42.9 us
    reduce_scatter x1, waiting for transfers between devices, local(): lax.psum_scatter(key_grad.astype(jnp.bfloat16), 'seq', scatter_dimension=...  42.4 us
    reduce_scatter x1, waiting for transfers between devices, local(): lax.psum_scatter(query_grad.astype(jnp.bfloat16), 'seq', scatter_dimensio...  42.1 us
  transfers between devices with their start and end apart: 21, of which 20 were waited for; matrix products, arithmetic and copies ran while one was open for 18% of the time, Pallas kernels for 0%

commit v1 on v0

--- a/solution.py
+++ b/solution.py
@@ -12,6 +12,28 @@
 norm_eps = 1e-05
 group_eps = 1.0
 highest_precision_mode = lax.Precision.HIGHEST
+
+
+def laid_out(blocks, dim):
+    dims = list(blocks.shape[1:])
+    dims[dim] *= blocks.shape[0]
+    return jnp.moveaxis(blocks, 0, dim).reshape(dims)
+
+
+def grow_blocks(shard, axis):
+    size = lax.axis_size(axis)
+    pieces = shard[None]
+    for level in range(size.bit_length() - 1):
+        bit = 1 << level
+        other = lax.ppermute(pieces, axis, [(i, i ^ bit) for i in range(size)])
+        both = jnp.stack([pieces, other])
+        upper = lax.axis_index(axis) >> level & 1
+        pieces = jnp.where(upper == 0, both, both[::-1]).reshape(-1, *shard.shape)
+    return pieces
+
+
+def collect(array, axis, dim):
+    return laid_out(grow_blocks(array, axis), dim)
 
 
 def entering(array, axis, join, neutral, backward):
@@ -38,7 +60,7 @@
 
 
 def feature_gather(tensor):
-    return lax.all_gather(tensor, "tp", axis=1, tiled=True)
+    return collect(tensor, "tp", 1)
 
 
 def feature_sum(tensor):

time: 1430 us -> 1550 us (1.084)
  starting transfers between devices: 2.22 us -> 45.8 us
  local copies, waits for them, and re-layouts: 79.9 us -> 116 us
  other arithmetic: 90.3 us -> 113 us
    ppermute x0 -> x8, waiting for transfers between devices: none -> 372 us  [grow_blocks(): other = lax.ppermute(pieces, axis, [(i, i ^ bit) for i in range(size)])]
    all_gather x4 -> x0, waiting for transfers between devices: 296 us -> none  [feature_gather(): return lax.all_gather(tensor, 'tp', axis=1, tiled=True)]
    ppermute x0 -> x8, starting transfers between devices: none -> 44.8 us  [grow_blocks(): other = lax.ppermute(pieces, axis, [(i, i ^ bit) for i in range(size)])]
    reshape x0 -> x5, local copies, waits for them, and re-layouts: none -> 31.7 us  [the longest x3 18.8 us: grow_blocks(): pieces = jnp.where(upper == 0, both, both[::-1]).reshape(-1, *shard.shape)]
    all_gather x1, waiting for transfers between devices: 23.2 us -> 0.02 us  [local(): lax.all_gather(value_weight, 'seq', axis=0, tiled=True)]
    another operation x1 -> x16, other arithmetic: 3.68 us -> 25.8 us  [the longest x15 24.3 us: grow_blocks(): both = jnp.stack([pieces, other])]
    reduce_scatter x4, waiting for transfers between devices: 279 us -> 260 us  [feature_sum(): lax.psum_scatter(tensor.astype(jnp.bfloat16), 'tp', scatter_dimension=1,...]
    all_gather x1, waiting for transfers between devices: 17.9 us -> 0.01 us  [local(): lax.all_gather(query_weight, 'seq', axis=0, tiled=True)]
  transfers between devices with their start and end apart: 21 -> 25, of which waited for: 20 -> 20; matrix products, arithmetic and copies ran while one was open for 18% -> 19% of each run, Pallas kernels for 0% -> 0%
where the time goes in v1:
time: 1550 us; the launch traced here: 1540 us
  waiting for transfers between devices  947 us (61%)
  matrix products  224 us (14%)
  local copies, waits for them, and re-layouts  116 us (7%)
  other arithmetic  113 us (7%)
  blocking collectives  80.8 us (5%)
  starting transfers between devices  45.8 us (3%)
    ppermute x8, waiting for transfers between devices, grow_blocks(): other = lax.ppermute(pieces, axis, [(i, i ^ bit) for i in range(size)])  372 us
    reduce_scatter x4, waiting for transfers between devices, feature_sum(): lax.psum_scatter(tensor.astype(jnp.bfloat16), 'tp', scatter_dimension=1,...  260 us
    psum x4, blocking collectives, row_totals(): return lax.psum((linear, squared), 'tp')  58.7 us
    reduce_scatter x1, waiting for transfers between devices, local(): lax.psum_scatter(out_grad.astype(jnp.bfloat16), 'seq', scatter_dimension=...  52.6 us
    reduce_scatter x1, waiting for transfers between devices, local(): lax.psum_scatter(value_grad.astype(jnp.bfloat16), 'seq', scatter_dimensio...  52.6 us
    reduce_scatter x1, waiting for transfers between devices, local(): lax.psum_scatter(gate_grad.astype(jnp.bfloat16), 'seq', scatter_dimension...  52.3 us
    ppermute x8, starting transfers between devices, grow_blocks(): other = lax.ppermute(pieces, axis, [(i, i ^ bit) for i in range(size)])  44.8 us
    reduce_scatter x1, waiting for transfers between devices, local(): lax.psum_scatter(key_grad.astype(jnp.bfloat16), 'seq', scatter_dimension=...  42.1 us
  transfers between devices with their start and end apart: 25, of which 20 were waited for; matrix products, arithmetic and copies ran while one was open for 19% of the time, Pallas kernels for 0%

profile of v1, /device:TPU:0, one launch (start us, length us, event | category | flops | bytes accessed | tf_op | source)
XLA Modules:
  0.0 1543.4 jit_solution(11771696655694867694)
XLA Ops:
  11.1 13.7 all-reduce.4
  26.3 22.9 %collective-permute-done = bf16[1,1024,512]{2,1,0:T(8,128)(2,1)S(1)} collective-permute-done((bf16[1,1024,512]{2,1,0:T(8,128)(2,1)}, bf16[1,1024,512]{2,1,0:T(8,128)(2,1)S(1)}, u32[]{:S(2)}, u32[]{:S(2)}) %collective-permute-start) | collective-permute-done | bytes 1048608 | tf_op jit(solution)/shard_map/ppermute | solution.py:28
  54.0 88.4 %collective-permute-done.1 = bf16[2,1024,512]{2,1,0:T(8,128)(2,1)} collective-permute-done((bf16[2,1024,512]{2,1,0:T(8,128)(2,1)}, bf16[2,1024,512]{2,1,0:T(8,128)(2,1)}, u32[]{:S(2)}, u32[]{:S(2)}) %collective-permute-start.1) | collective-permute-done | bytes 2097184 | tf_op jit(solution)/shard_map/ppermute | solution.py:28
  147.8 5.2 copy.113
  153.1 7.9 reshape.520
  161.0 4.9 copy.182
  173.8 5.4 fusion.94
  183.3 9.6 convolution_convert_fusion.10
  197.5 5.1 fusion.50
  204.2 5.0 while.58
  211.4 8.8 all-gather.1
  227.9 17.3 %all-gather.22.cloned.1.call-done = bf16[16,256,512]{2,1,0:T(8,128)(2,1)} async-done(((bf16[2,256,512]{2,1,0:T(8,128)(2,1)}), bf16[16,256,512]{2,1,0:T(8,128)(2,1)}) %all-gather.22.cloned.1.call-update) | async-done | bytes 4194320 | tf_op jit(solution)/shard_map/all_gather | solution.py:44
  247.6 5.9 fusion.92
  253.5 7.4 copy.125
  267.4 16.2 %all-gather.10.cloned.1.call-done = bf16[2048,1024]{1,0:T(8,128)(2,1)} async-done(((bf16[256,1024]{1,0:T(8,128)(2,1)}), bf16[2048,1024]{1,0:T(8,128)(2,1)}) %all-gather.10.cloned.1.call-update) | async-done | bytes 4194320 | tf_op jit(solution)/shard_map/all_gather | solution.py:182
  283.5 12.0 multiply_convert_fusion.2
  295.5 27.1 %all-gather.18.cloned.1.call-done = bf16[1024,2048]{1,0:T(8,128)(2,1)} async-done(((bf16[1024,256]{1,0:T(8,128)(2,1)}), bf16[1024,2048]{1,0:T(8,128)(2,1)}) %all-gather.18.cloned.1.call-update) | async-done | bytes 4194320 | tf_op jit(solution)/shard_map/all_gather | solution.py:183
  322.6 8.3 convolution_convert_fusion.7
  333.6 62.6 %collective-permute-done.4 = bf16[1,1024,512]{2,1,0:T(8,128)(2,1)S(1)} collective-permute-done((bf16[1,1024,512]{2,1,0:T(8,128)(2,1)S(1)}, bf16[1,1024,512]{2,1,0:T(8,128)(2,1)S(1)}, u32[]{:S(2)}, u32[]{:S(2)}) %collective-permute-start.4) | collective-permute-done | bytes 1048608 | tf_op jit(solution)/shard_map/ppermute | solution.py:28
  398.9 52.6 %reduce-scatter.10.cloned.1.call-done = bf16[1024,512]{1,0:T(8,128)(2,1)} async-done(((bf16[1024,2048]{1,0:T(8,128)(2,1)}), bf16[1024,512]{1,0:T(8,128)(2,1)}) %reduce-scatter.10.cloned.1.call-update) | async-done | bytes 1048592 | tf_op jit(solution)/shard_map/reduce_scatter | solution.py:67
  453.3 21.9 %all-reduce.3 = (f32[1024]{0:T(1024)S(1)}, f32[1024]{0:T(1024)S(1)}) all-reduce(f32[1024]{0:T(1024)S(1)} %get-tuple-element.352, f32[1024]{0:T(1024)S(1)} %get-tuple-element.351), channel_id=1, replica_groups=mesh['seq'=8,'tp'=4] {'tp'}, use_global_device_ids=true, to_apply=%region_14.15 | all-reduce | flops 2048 | bytes 16384 | tf_op jit(solution)/shard_map/psum | solution.py:73
  475.8 35.5 %collective-permute-start.2 = (bf16[1,1024,512]{2,1,0:T(8,128)(2,1)S(1)}, bf16[1,1024,512]{2,1,0:T(8,128)(2,1)S(1)}, u32[]{:S(2)}, u32[]{:S(2)}) collective-permute-start(bf16[1,1024,512]{2,1,0:T(8,128)(2,1)S(1)} %get-tuple-element.424), channel_id=1, source_target_pairs={{0,1},{1,0},{2,3},{3,2},{4,5},{5,4},{6,7},{7,6},{8,9},{9,8},{10,11... | collective-permute-start | bytes 3145736 | tf_op jit(solution)/shard_map/ppermute | solution.py:28
  511.3 22.1 %collective-permute-done.2 = bf16[1,1024,512]{2,1,0:T(8,128)(2,1)S(1)} collective-permute-done((bf16[1,1024,512]{2,1,0:T(8,128)(2,1)S(1)}, bf16[1,1024,512]{2,1,0:T(8,128)(2,1)S(1)}, u32[]{:S(2)}, u32[]{:S(2)}) %collective-permute-start.2) | collective-permute-done | bytes 1048608 | tf_op jit(solution)/shard_map/ppermute | solution.py:28
  544.2 6.2 copy.135
  550.4 10.1 fusion.99
  560.5 67.6 %collective-permute-done.3 = bf16[2,1024,512]{2,1,0:T(8,128)(2,1)} collective-permute-done((bf16[2,1024,512]{2,1,0:T(8,128)(2,1)}, bf16[2,1024,512]{2,1,0:T(8,128)(2,1)}, u32[]{:S(2)}, u32[]{:S(2)}) %collective-permute-start.3) | collective-permute-done | bytes 2097184 | tf_op jit(solution)/shard_map/ppermute | solution.py:28
  632.9 6.3 copy.129
  639.2 13.8 fusion.10
  654.3 6.6 convolution_convert_fusion.5
  661.0 10.5 convolution_convert_fusion.6
  671.6 65.5 %reduce-scatter.14.cloned.1.call-done = bf16[1024,512]{1,0:T(8,128)(2,1)} async-done(((bf16[1024,2048]{1,0:T(8,128)(2,1)}), bf16[1024,512]{1,0:T(8,128)(2,1)}) %reduce-scatter.14.cloned.1.call-update) | async-done | bytes 1048592 | tf_op jit(solution)/shard_map/reduce_scatter | solution.py:67
  740.6 11.5 all-reduce.2
  752.1 64.8 %reduce-scatter.12.cloned.1.call-done = bf16[1024,512]{1,0:T(8,128)(2,1)} async-done(((bf16[1024,2048]{1,0:T(8,128)(2,1)}), bf16[1024,512]{1,0:T(8,128)(2,1)}) %reduce-scatter.12.cloned.1.call-update) | async-done | bytes 1048592 | tf_op jit(solution)/shard_map/reduce_scatter | solution.py:67
  823.5 23.2 %collective-permute-done.6 = bf16[1,1024,512]{2,1,0:T(8,128)(2,1)S(1)} collective-permute-done((bf16[1,1024,512]{2,1,0:T(8,128)(2,1)S(1)}, bf16[1,1024,512]{2,1,0:T(8,128)(2,1)S(1)}, u32[]{:S(2)}, u32[]{:S(2)}) %collective-permute-start.6) | collective-permute-done | bytes 1048608 | tf_op jit(solution)/shard_map/ppermute | solution.py:28
  856.4 85.4 %collective-permute-done.7 = bf16[2,1024,512]{2,1,0:T(8,128)(2,1)} collective-permute-done((bf16[2,1024,512]{2,1,0:T(8,128)(2,1)}, bf16[2,1024,512]{2,1,0:T(8,128)(2,1)}, u32[]{:S(2)}, u32[]{:S(2)}) %collective-permute-start.7) | collective-permute-done | bytes 2097184 | tf_op jit(solution)/shard_map/ppermute | solution.py:28
  946.7 6.3 copy.140
  953.0 14.5 fusion.80
  967.4 5.4 copy.142
  986.3 4.9 copy.145
  991.3 6.0 fusion.18
  998.9 5.4 while.59
  1007.4 8.5 convolution_convert_fusion.1
  1015.9 6.7 convolution_convert_fusion
  1039.5 6.3 convolution_convert_fusion.9
  1045.9 9.4 convolution_convert_fusion.2
  1055.4 9.4 convolution_convert_fusion.3
  1065.1 14.8 while.57
  1087.7 6.0 convolution_convert_fusion.8
  1098.6 7.5 fusion.54
  1113.7 6.3 convolution_convert_fusion.4
  1121.3 7.4 fusion.95
  1128.6 7.1 fusion.98
  1135.7 6.9 fusion.97
  1142.6 13.2 add_convert_fusion
  1155.8 18.3 %all-reduce.9.cloned.1.call-done = (bf16[2048,1024]{1,0:T(8,128)(2,1)}, bf16[1024,2048]{1,0:T(8,128)(2,1)}) async-done(((bf16[2048,1024]{1,0:T(8,128)(2,1)}, bf16[1024,2048]{1,0:T(8,128)(2,1)}), (bf16[2048,1024]{1,0:T(8,128)(2,1)}, bf16[1024,2048]{1,0:T(8,128)(2,1)})) %all-reduce.9.cloned.1.call-update) | async-done | bytes 8388624 | tf_op jit(solution)/shard_map/psum | solution.py:362
  1174.1 6.8 convert_element_type.328
  1185.3 33.2 %reduce-scatter.18.cloned.1.call-done = bf16[256,512]{1,0:T(8,128)(2,1)} async-done(((bf16[2048,512]{1,0:T(8,128)(2,1)}), bf16[256,512]{1,0:T(8,128)(2,1)}) %reduce-scatter.18.cloned.1.call-update) | async-done | bytes 262160 | tf_op jit(solution)/shard_map/reduce_scatter | solution.py:345
  1220.3 52.6 %reduce-scatter.26.cloned.1.call-done = bf16[1024,256]{1,0:T(8,128)(2,1)} async-done(((bf16[1024,2048]{1,0:T(8,128)(2,1)}), bf16[1024,256]{1,0:T(8,128)(2,1)}) %reduce-scatter.26.cloned.1.call-update) | async-done | bytes 524304 | tf_op jit(solution)/shard_map/reduce_scatter | solution.py:357
  1275.0 52.3 %reduce-scatter.24.cloned.1.call-done = bf16[256,1024]{1,0:T(8,128)(2,1)} async-done(((bf16[2048,1024]{1,0:T(8,128)(2,1)}), bf16[256,1024]{1,0:T(8,128)(2,1)}) %reduce-scatter.24.cloned.1.call-update) | async-done | bytes 524304 | tf_op jit(solution)/shard_map/reduce_scatter | solution.py:354
  1329.5 42.1 %reduce-scatter.20.cloned.1.call-done = bf16[256,512]{1,0:T(8,128)(2,1)} async-done(((bf16[2048,512]{1,0:T(8,128)(2,1)}), bf16[256,512]{1,0:T(8,128)(2,1)}) %reduce-scatter.20.cloned.1.call-update) | async-done | bytes 262160 | tf_op jit(solution)/shard_map/reduce_scatter | solution.py:348
  1373.4 52.6 %reduce-scatter.22.cloned.1.call-done = bf16[256,1024]{1,0:T(8,128)(2,1)} async-done(((bf16[2048,1024]{1,0:T(8,128)(2,1)}), bf16[256,1024]{1,0:T(8,128)(2,1)}) %reduce-scatter.22.cloned.1.call-update) | async-done | bytes 524304 | tf_op jit(solution)/shard_map/reduce_scatter | solution.py:351
  1428.1 76.8 %reduce-scatter.16.cloned.1.call-done = bf16[1024,512]{1,0:T(8,128)(2,1)} async-done(((bf16[1024,2048]{1,0:T(8,128)(2,1)}), bf16[1024,512]{1,0:T(8,128)(2,1)}) %reduce-scatter.16.cloned.1.call-update) | async-done | bytes 1048592 | tf_op jit(solution)/shard_map/reduce_scatter | solution.py:67
  1507.6 13.3 all-reduce.5
  1522.0 11.6 all-reduce.1
  (321 shorter events, 203.5 us)
Async XLA Ops:
  7.2 17.7 %copy-start.1 = (bf16[1024,512]{1,0:T(8,128)(2,1)S(1)}, bf16[1024,512]{1,0:T(8,128)(2,1)}, u32[]{:S(2)}) copy-start(bf16[1024,512]{1,0:T(8,128)(2,1)} %param.19) | copy-start | bytes 3145732
  7.2 17.7 %copy-start.66 = (f32[512]{0:T(512)S(1)}, f32[512]{0:T(512)}, u32[]{:S(2)}) copy-start(f32[512]{0:T(512)} %param.20) | copy-start | bytes 6148
  7.2 158.8 %all-gather.16.cloned.1.call-start = ((), (), s32[]{:S(2)}) async-start(), calls=%async_computation.12 | async-start | bytes 2359296 | tf_op jit(solution)/shard_map/all_gather | solution.py:180
  7.9 162.0 %all-gather.14.cloned.1.call-start = ((), (), s32[]{:S(2)}) async-start(), calls=%async_computation.11 | async-start | bytes 2359296 | tf_op jit(solution)/shard_map/all_gather | solution.py:179
  8.7 174.6 %all-gather.12.cloned.1.call-start = ((), (), s32[]{:S(2)}) async-start(), calls=%async_computation.10 | async-start | bytes 4718592 | tf_op jit(solution)/shard_map/all_gather | solution.py:181
  9.4 235.7 %all-gather.22.cloned.1.call-start = ((), (), s32[]{:S(2)}) async-start(), calls=%async_computation.24 | async-start | bytes 4718592 | tf_op jit(solution)/shard_map/all_gather | solution.py:44
  26.3 22.9 %collective-permute-start = (bf16[1,1024,512]{2,1,0:T(8,128)(2,1)}, bf16[1,1024,512]{2,1,0:T(8,128)(2,1)S(1)}, u32[]{:S(2)}, u32[]{:S(2)}) collective-permute-start(bf16[1,1024,512]{2,1,0:T(8,128)(2,1)} %get-tuple-element.437), channel_id=1, source_target_pairs={{0,1},{1,0},{2,3},{3,2},{4,5},{5,4},{6,7},{7,6},{8,9},{9,8},{10,11... | collective-permute-start | bytes 3145736 | tf_op jit(solution)/shard_map/ppermute | solution.py:28
  52.0 90.5 %collective-permute-start.1 = (bf16[2,1024,512]{2,1,0:T(8,128)(2,1)}, bf16[2,1024,512]{2,1,0:T(8,128)(2,1)}, u32[]{:S(2)}, u32[]{:S(2)}) collective-permute-start(bf16[2,1024,512]{2,1,0:T(8,128)(2,1)} %get-tuple-element.435), channel_id=1, source_target_pairs={{0,2},{1,3},{2,0},{3,1},{4,6},{5,7},{6,4},{7,5},{8,10},{9,11},{10,... | collective-permute-start | bytes 6291464 | tf_op jit(solution)/shard_map/ppermute | solution.py:28
  52.1 145.4 %copy-start.59 = (f32[512,2]{0,1:T(2,128)}, f32[512,2]{0,1:T(2,128)S(1)}, u32[]{:S(2)}) copy-start(f32[512,2]{0,1:T(2,128)S(1)} %get-tuple-element.448) | copy-start | bytes 12292
  54.0 127.6 %copy-start.39 = (f32[1024,128]{1,0:T(8,128)}, f32[1024,128]{1,0:T(8,128)S(1)}, u32[]{:S(2)}) copy-start(f32[1024,128]{1,0:T(8,128)S(1)} %get-tuple-element.440) | copy-start | bytes 1572868
  54.0 127.6 %copy-start.42 = (f32[1024,128]{1,0:T(8,128)}, f32[1024,128]{1,0:T(8,128)S(1)}, u32[]{:S(2)}) copy-start(f32[1024,128]{1,0:T(8,128)S(1)} %get-tuple-element.441) | copy-start | bytes 1572868
  173.8 5.4 copy-start.49
  173.8 5.4 copy-start.56
  183.3 38.7 %copy-start.16 = (bf16[2,512,2,256]{3,1,2,0:T(8,128)(2,1)}, bf16[2,512,2,256]{3,1,2,0:T(8,128)(2,1)S(1)}, u32[]{:S(2)}) copy-start(bf16[2,512,2,256]{3,1,2,0:T(8,128)(2,1)S(1)} %fusion.48) | copy-start | bytes 3145732
  210.2 73.3 %all-gather.10.cloned.1.call-start = ((), (), s32[]{:S(2)}) async-start(), calls=%async_computation.9 | async-start | bytes 4718592 | tf_op jit(solution)/shard_map/all_gather | solution.py:182
  210.8 111.9 %all-gather.18.cloned.1.call-start = ((), (), s32[]{:S(2)}) async-start(), calls=%async_computation.13 | async-start | bytes 4718592 | tf_op jit(solution)/shard_map/all_gather | solution.py:183
  211.3 240.2 %reduce-scatter.10.cloned.1.call-start = ((), (), s32[]{:S(2)}) async-start(), calls=%async_computation.14 | async-start | bytes 5242880 | tf_op jit(solution)/shard_map/reduce_scatter | solution.py:67
  245.4 8.0 copy-start.14
  295.5 35.4 %copy-start.57 = (bf16[1024,1024]{0,1:T(8,128)(2,1)}, bf16[1024,1024]{0,1:T(8,128)(2,1)S(1)}, u32[]{:S(2)}) copy-start(bf16[1024,1024]{0,1:T(8,128)(2,1)S(1)} %get-tuple-element.452) | copy-start | bytes 6291460
  330.9 406.2 %reduce-scatter.14.cloned.1.call-start = ((), (), s32[]{:S(2)}) async-start(), calls=%async_computation.16 | async-start | bytes 5242880 | tf_op jit(solution)/shard_map/reduce_scatter | solution.py:67
  332.1 64.1 %collective-permute-start.4 = (bf16[1,1024,512]{2,1,0:T(8,128)(2,1)S(1)}, bf16[1,1024,512]{2,1,0:T(8,128)(2,1)S(1)}, u32[]{:S(2)}, u32[]{:S(2)}) collective-permute-start(bf16[1,1024,512]{2,1,0:T(8,128)(2,1)S(1)} %bitcast.275), channel_id=1, source_target_pairs={{0,1},{1,0},{2,3},{3,2},{4,5},{5,4},{6,7},{7,6},{8,9},{9,8},{10,11... | collective-permute-start | bytes 3145736 | tf_op jit(solution)/shard_map/ppermute | solution.py:28
  398.9 76.4 %copy-start.68 = (f32[512]{0:T(512)S(1)}, f32[512]{0:T(512)}, u32[]{:S(2)}) copy-start(f32[512]{0:T(512)} %param.26) | copy-start | bytes 6148
  398.9 140.5 %collective-permute-start.5 = (bf16[2,1024,512]{2,1,0:T(8,128)(2,1)}, bf16[2,1024,512]{2,1,0:T(8,128)(2,1)}, u32[]{:S(2)}, u32[]{:S(2)}) collective-permute-start(bf16[2,1024,512]{2,1,0:T(8,128)(2,1)} %get-tuple-element.431), channel_id=1, source_target_pairs={{0,2},{1,3},{2,0},{3,1},{4,6},{5,7},{6,4},{7,5},{8,10},{9,11},{10,... | collective-permute-start | bytes 6291464 | tf_op jit(solution)/shard_map/ppermute | solution.py:28
  451.5 23.8 %copy-start.28 = (bf16[1024,512]{1,0:T(8,128)(2,1)S(1)}, bf16[1024,512]{1,0:T(8,128)(2,1)}, u32[]{:S(2)}) copy-start(bf16[1024,512]{1,0:T(8,128)(2,1)} %reduce-scatter.10.cloned.1.call-done) | copy-start | bytes 3145732
  475.8 57.6 %collective-permute-start.2 = (bf16[1,1024,512]{2,1,0:T(8,128)(2,1)S(1)}, bf16[1,1024,512]{2,1,0:T(8,128)(2,1)S(1)}, u32[]{:S(2)}, u32[]{:S(2)}) collective-permute-start(bf16[1,1024,512]{2,1,0:T(8,128)(2,1)S(1)} %get-tuple-element.424), channel_id=1, source_target_pairs={{0,1},{1,0},{2,3},{3,2},{4,5},{5,4},{6,7},{7,6},{8,9},{9,8},{10,11... | collective-permute-start | bytes 3145736 | tf_op jit(solution)/shard_map/ppermute | solution.py:28
  533.6 5.8 copy-start.37
  536.2 91.9 %collective-permute-start.3 = (bf16[2,1024,512]{2,1,0:T(8,128)(2,1)}, bf16[2,1024,512]{2,1,0:T(8,128)(2,1)}, u32[]{:S(2)}, u32[]{:S(2)}) collective-permute-start(bf16[2,1024,512]{2,1,0:T(8,128)(2,1)} %get-tuple-element.433), channel_id=1, source_target_pairs={{0,2},{1,3},{2,0},{3,1},{4,6},{5,7},{6,4},{7,5},{8,10},{9,11},{10,... | collective-permute-start | bytes 6291464 | tf_op jit(solution)/shard_map/ppermute | solution.py:28
  550.4 77.7 %copy-start.38 = (bf16[1,2,1024,512]{3,2,1,0:T(8,128)(2,1)S(1)}, bf16[1,2,1024,512]{3,2,1,0:T(8,128)(2,1)}, u32[]{:S(2)}) copy-start(bf16[1,2,1024,512]{3,2,1,0:T(8,128)(2,1)} %get-tuple-element.432) | copy-start | bytes 6291460
  639.2 15.1 copy-start.71
  660.9 156.0 %reduce-scatter.12.cloned.1.call-start = ((), (), s32[]{:S(2)}) async-start(), calls=%async_computation.15 | async-start | bytes 5242880 | tf_op jit(solution)/shard_map/reduce_scatter | solution.py:67
  671.5 393.4 %all-gather.20.cloned.1.call-start = ((), (), s32[]{:S(2)}) async-start(), calls=%async_computation.17 | async-start | bytes 4718592 | tf_op jit(solution)/shard_map/all_gather | solution.py:44
  737.1 79.8 %copy-start.51 = (bf16[1024,512]{1,0:T(8,128)(2,1)S(1)}, bf16[1024,512]{1,0:T(8,128)(2,1)}, u32[]{:S(2)}) copy-start(bf16[1024,512]{1,0:T(8,128)(2,1)} %reduce-scatter.14.cloned.1.call-done) | copy-start | bytes 3145732
  821.9 24.8 %collective-permute-start.6 = (bf16[1,1024,512]{2,1,0:T(8,128)(2,1)S(1)}, bf16[1,1024,512]{2,1,0:T(8,128)(2,1)S(1)}, u32[]{:S(2)}, u32[]{:S(2)}) collective-permute-start(bf16[1,1024,512]{2,1,0:T(8,128)(2,1)S(1)} %convert_bitcast_fusion), channel_id=1, source_target_pairs={{0,1},{1,0},{2,3},{3,2},{4,5},{5,4},{6,7},{7,6},{8,9},{9,8},{10,11... | collective-permute-start | bytes 3145736 | tf_op jit(solution)/shard_map/ppermute | solution.py:28
  848.7 93.0 %collective-permute-start.7 = (bf16[2,1024,512]{2,1,0:T(8,128)(2,1)}, bf16[2,1024,512]{2,1,0:T(8,128)(2,1)}, u32[]{:S(2)}, u32[]{:S(2)}) collective-permute-start(bf16[2,1024,512]{2,1,0:T(8,128)(2,1)} %get-tuple-element.428), channel_id=1, source_target_pairs={{0,2},{1,3},{2,0},{3,1},{4,6},{5,7},{6,4},{7,5},{8,10},{9,11},{10,... | collective-permute-start | bytes 6291464 | tf_op jit(solution)/shard_map/ppermute | solution.py:28
  972.8 4.6 copy-start.8
  972.8 5.9 copy-start.9
  991.3 6.0 copy-start.11
  1007.3 166.8 %all-reduce.9.cloned.1.call-start = ((), (), s32[]{:S(2)}) async-start(), calls=%async_computation.25 | async-start | bytes 16777216 | tf_op jit(solution)/shard_map/psum | solution.py:362
  1007.4 8.5 copy-start.48
  1007.4 8.5 copy-start.73
  1022.7 5.5 copy-start.4
  1022.7 195.8 %reduce-scatter.18.cloned.1.call-start = ((), (), s32[]{:S(2)}) async-start(), calls=%async_computation.19 | async-start | bytes 2359296 | tf_op jit(solution)/shard_map/reduce_scatter | solution.py:345
  1023.9 4.3 copy-start.6
  1023.9 4.3 copy-start.12
  1045.9 227.1 %reduce-scatter.26.cloned.1.call-start = ((), (), s32[]{:S(2)}) async-start(), calls=%async_computation.23 | async-start | bytes 4718592 | tf_op jit(solution)/shard_map/reduce_scatter | solution.py:357
  1055.4 272.0 %reduce-scatter.24.cloned.1.call-start = ((), (), s32[]{:S(2)}) async-start(), calls=%async_computation.22 | async-start | bytes 4718592 | tf_op jit(solution)/shard_map/reduce_scatter | solution.py:354
  1064.8 306.7 %reduce-scatter.20.cloned.1.call-start = ((), (), s32[]{:S(2)}) async-start(), calls=%async_computation.20 | async-start | bytes 2359296 | tf_op jit(solution)/shard_map/reduce_scatter | solution.py:348
  1065.0 14.9 copy-start.65
  1093.7 332.3 %reduce-scatter.22.cloned.1.call-start = ((), (), s32[]{:S(2)}) async-start(), calls=%async_computation.21 | async-start | bytes 4718592 | tf_op jit(solution)/shard_map/reduce_scatter | solution.py:351
  1110.0 3.7 copy-start.27
  1120.0 8.6 copy-start.53
  1120.1 384.9 %reduce-scatter.16.cloned.1.call-start = ((), (), s32[]{:S(2)}) async-start(), calls=%async_computation.18 | async-start | bytes 5242880 | tf_op jit(solution)/shard_map/reduce_scatter | solution.py:67
  1121.3 7.4 copy-start.50
  1128.6 7.1 copy-start.55
  1128.6 7.1 copy-start.72
  1135.7 6.9 copy-start.36
  1135.7 6.9 copy-start.47
  1174.1 6.8 copy-start.45
  1275.0 229.9 %copy-start.2 = (bf16[1024,512]{1,0:T(8,128)(2,1)S(1)}, bf16[1024,512]{1,0:T(8,128)(2,1)}, u32[]{:S(2)}) copy-start(bf16[1024,512]{1,0:T(8,128)(2,1)} %param.19) | copy-start | bytes 3145732
  1275.0 229.9 %copy-start.62 = (f32[1024]{0:T(1024)S(1)}, f32[1024]{0:T(1024)}, u32[]{:S(2)}) copy-start(f32[1024]{0:T(1024)} %copy-done.61) | copy-start | bytes 12292
  1275.0 229.9 %copy-start.64 = (f32[1024]{0:T(1024)S(1)}, f32[1024]{0:T(1024)}, u32[]{:S(2)}) copy-start(f32[1024]{0:T(1024)} %copy-done.63) | copy-start | bytes 12292
  1275.0 229.9 %copy-start.67 = (f32[512]{0:T(512)S(1)}, f32[512]{0:T(512)}, u32[]{:S(2)}) copy-start(f32[512]{0:T(512)} %param.20) | copy-start | bytes 6148
  1329.5 178.1 %copy-start.69 = (bf16[512]{0:T(512)(128)(2,1)S(1)}, bf16[512]{0:T(512)(128)(2,1)}, u32[]{:S(2)}) copy-start(bf16[512]{0:T(512)(128)(2,1)} %get-tuple-element.347) | copy-start | bytes 3076
  1329.5 204.2 %copy-start.21 = (f32[1024,512]{1,0:T(8,128)S(1)}, f32[1024,512]{1,0:T(8,128)}, u32[]{:S(2)}) copy-start(f32[1024,512]{1,0:T(8,128)} %copy-done.20) | copy-start | bytes 6291460
  (38 other events, 78.5 us)
Sparse Core Ops, SparseCore 0:
  9.9 30.4 all-gather.15
  42.3 27.8 all-gather.13
  72.1 36.5 all-gather.11
  210.3 34.8 all-gather.21
  246.9 36.5 all-gather.9
  285.2 37.3 all-gather.17
  331.1 120.4 reduce-scatter.9
  661.1 76.0 reduce-scatter.13
  739.4 77.4 reduce-scatter.11
  1007.4 36.6 all-gather.19
  1047.9 126.1 all-reduce.8
  1177.2 41.2 reduce-scatter.17
  1221.9 51.0 reduce-scatter.25
  1276.2 51.1 reduce-scatter.23
  1330.5 41.0 reduce-scatter.19
  1374.8 51.1 reduce-scatter.21
  1428.1 76.7 reduce-scatter.15
